TPU v7x, 32 devices: a whole 2x2x4 slice. The times are simulated.
32 devices in a mesh: sta: 8 (over z, y), seg: 4 (over x, core).
Axes of the slice: x: 2, y: 2, z: 4, core: 2. Of those that a mesh axis runs over, the one named last changes fastest.
Arguments:
- spectra: bfloat16 [48, 16, 2, 1024], P('sta', 'seg'), may hold values from -6 to 6
- observed: float32 [40, 6, 6, 512], P('sta'), may hold values from -8 to 8
- pair_table: int32 [40, 2], P('sta'), may hold values from -1 to 7, as said below
Outputs:
- gradient: float32 [48, 2, 1024], P('sta', None, 'seg')
Inputs may be any that keep to these rules, and one draw needn't show every extreme that they name: `pair_table`: rows are slots; each unordered pair of station blocks p <= q of the 8 blocks stands in exactly one row as (p, q); every other row is (-1, -1).
All inputs are finite; a program needn't handle non-finite values.
Results may differ from a plain program's by a relative error of at most 0.0013.
Values may be sent and summed in bfloat16 or wider, within the bound.
No kernel may reach another device: no remote copies, remote signals or barrier semaphores. Data moves between devices by JAX's collectives and lax.ppermute only.
A program may use at most 64 MiB of HBM per device.

v0:
```python
import math
import jax
import jax.numpy as jnp
from jax import lax
from jax.sharding import PartitionSpec as P

F = 1024
LAGS = 512


def lag_kernel(start, count):
    frequency = (start + jnp.arange(count, dtype=jnp.int32))[:, None]
    offset = jnp.arange(LAGS, dtype=jnp.int32)[None, :] - LAGS // 2
    phase = jnp.mod(frequency * offset, 2 * F)
    angle = math.pi / F * phase.astype(jnp.float32)
    return jnp.stack([jnp.cos(angle), -jnp.sin(angle)], axis=0).astype(jnp.bfloat16)


def group_cross(left, right, groups):
    station_count = left.shape[0]
    left = left.reshape(station_count, groups, -1, 2, left.shape[-1]).astype(jnp.float32)
    right = right.reshape(station_count, groups, -1, 2, right.shape[-1]).astype(jnp.float32)
    left_real = left[:, :, :, 0][:, None]
    left_imag = left[:, :, :, 1][:, None]
    right_real = right[:, :, :, 0][None]
    right_imag = right[:, :, :, 1][None]
    cross_real = jnp.sum(left_real * right_real + left_imag * right_imag, axis=3)
    cross_imag = jnp.sum(left_imag * right_real - left_real * right_imag, axis=3)
    return jnp.stack([cross_real, cross_imag], axis=3).astype(jnp.bfloat16)


def slot_cross(gathered, starts_all, station_count, groups):

    def one_slot(starts):
        left = lax.dynamic_slice_in_dim(gathered, starts[0], station_count, 0)
        right = lax.dynamic_slice_in_dim(gathered, starts[1], station_count, 0)
        return group_cross(left, right, groups)

    return lax.map(one_slot, starts_all)


def pair_mask(first, second, station_count):
    row_index = jnp.arange(station_count)[:, None]
    col_index = jnp.arange(station_count)[None, :]
    keep = (first >= 0)[..., None, None] & (
        (first != second)[..., None, None] | (row_index < col_index)
    )
    return keep.astype(jnp.float32)


def adjoint_terms(gamma, stacked):
    gamma_real = gamma[..., 0, :]
    gamma_imag = gamma[..., 1, :]
    stack_real = stacked[..., 0, :]
    stack_imag = stacked[..., 1, :]
    common = gamma_real * stack_real + gamma_imag * stack_imag
    twist = gamma_imag * stack_real - gamma_real * stack_imag
    left_term = jnp.stack([common.sum(-2), twist.sum(-2)], axis=-2)
    right_term = jnp.stack([common.sum(-3), -twist.sum(-3)], axis=-2)
    return (left_term, right_term)


def on_device(spectra, observed, pair_table):
    station_dev = spectra.shape[0]
    slot_count = pair_table.shape[0]
    seg_devices = lax.axis_size("seg")
    scale = 1.0 / math.sqrt(F * spectra.shape[1] * seg_devices)
    first = pair_table[:, 0]
    second = pair_table[:, 1]
    starts_all = jnp.maximum(pair_table, 0) * station_dev
    keep = pair_mask(first, second, station_dev).reshape(-1, 1)
    observe_flat = observed.reshape(-1, LAGS)
    local = lax.all_to_all(spectra, "seg", split_axis=3, concat_axis=1, tiled=True)
    gathered = lax.all_gather(local, "sta", axis=0, tiled=True)
    width = local.shape[3]
    crossed = slot_cross(gathered, starts_all, station_dev, seg_devices)
    stacked = jnp.sum(lax.optimization_barrier(crossed).astype(jnp.float32), axis=3)
    kernel = lag_kernel(lax.axis_index("seg") * width, width)
    exact = lax.optimization_barrier(kernel).astype(jnp.float32)
    lag_terms = jnp.dot(
        stacked.reshape(-1, 2 * width),
        exact.reshape(2 * width, LAGS),
        precision=lax.Precision.HIGHEST,
    )
    lag_sum = lax.psum(lag_terms, "seg")
    residual = (keep * jnp.tanh(scale * lag_sum - observe_flat)).astype(jnp.bfloat16)
    matrix = kernel.reshape(2 * width, LAGS)
    gamma = scale * lax.dot_general(
        residual, matrix, (((1,), (1,)), ((), ())), preferred_element_type=jnp.float32
    )
    gamma = gamma.reshape(slot_count, station_dev, station_dev, 2, width)
    left_term, right_term = adjoint_terms(gamma, stacked)
    blocks = lax.axis_size("sta")
    block_index = jnp.arange(blocks)[None, :]
    choose_left = (first[:, None] == block_index).astype(jnp.float32)
    choose_right = (second[:, None] == block_index).astype(jnp.float32)
    contract = (((0,), (0,)), ((), ()))
    buffer = lax.dot_general(
        choose_left, left_term.reshape(slot_count, -1), contract, precision=lax.Precision.HIGHEST
    )
    buffer = buffer + lax.dot_general(
        choose_right, right_term.reshape(slot_count, -1), contract, precision=lax.Precision.HIGHEST
    )
    buffer = buffer.reshape(blocks * station_dev, 2, width)
    result = lax.psum_scatter(buffer, "sta", scatter_dimension=0, tiled=True)
    return result


def solution(mesh):
    placed = (P("sta", "seg", None, None), P("sta", None, None, None), P("sta", None))
    return jax.shard_map(
        on_device, mesh=mesh, in_specs=placed, out_specs=P("sta", None, "seg"), check_vma=False
    )
```

profile of v0, /device:TPU:0, one launch (start us, length us, event | category | flops | bytes accessed | tf_op | source)
XLA Modules:
  0.0 208.0 jit_solution(6341141259934463326)
XLA Ops:
  6.5 2.7 %copy.23 = bf16[6,4,2,1024]{0,1,2,3:T(4,128)(2,1)S(1)} copy(bf16[6,4,2,1024]{3,2,1,0:T(2,128)(2,1)} %param.5) | data formatting | bytes 196608 | tf_op args[0]
  9.2 4.1 %reshape.288 = bf16[4,2,6144]{2,1,0:T(2,128)(2,1)} reshape(bf16[1024,2,4,6]{3,2,1,0:T(4,128)(2,1)S(1)} %bitcast.64) | data formatting | bytes 196608
  13.3 4.2 %all-to-all-start = ((bf16[4,2,6144]{2,1,0:T(2,128)(2,1)}), bf16[4,2,6144]{2,1,0:T(2,128)(2,1)S(1)}, u32[]{:S(2)}, u32[]{:S(2)}) async-start(bf16[4,2,6144]{2,1,0:T(2,128)(2,1)} %reshape.288), calls=%async_computation | async-start | bytes 196608 | tf_op jit(solution)/shard_map/all_to_all | solution.py:73
  17.6 2.5 %fusion.3 = (bf16[1,256,512]{2,1,0:T(8,128)(2,1)S(1)}, bf16[1,256,512]{2,1,0:T(8,128)(2,1)S(1)}) fusion(s32[512]{0:T(512)S(1)} %iota_add_fusion, s32[256]{0:T(256)S(1)} %iota_add_fusion.1), kind=kLoop, calls=%fused_computation.26 | loop fusion | flops 2228224 | bytes 527360 | tf_op jit(solution)/shard_map/cos | solution.py:16
  20.4 1.4 all-to-all-done
  21.9 4.8 %reshape.289 = bf16[1024,2,4,6]{3,2,1,0:T(4,128)(2,1)S(1)} reshape(bf16[4,2,6144]{2,1,0:T(2,128)(2,1)S(1)} %all-to-all-done) | data formatting | bytes 196608
  26.6 1.8 copy.24
  28.4 33.1 %all_gather.3 = bf16[48,16,2,256]{3,1,2,0:T(8,128)(2,1)S(1)} all-gather(bf16[6,16,2,256]{3,1,2,0:T(8,128)(2,1)S(1)} %all_to_all.16), channel_id=1, replica_groups=mesh['sta'=8,'seg'=4] {'sta'}, dimensions={0}, use_global_device_ids=true | all-gather | bytes 884736 | tf_op jit(solution)/shard_map/all_gather | solution.py:74
  61.6 28.5 %while.10 = (s32[]{:T(128)}, bf16[5,6,6,4,2,256]{5,3,2,1,4,0:T(4,128)(2,1)S(1)}, s32[5,2]{0,1:T(2,128)S(1)}, bf16[48,16,2,256]{3,1,0,2:T(8,128)(2,1)S(1)}, s32[]{:T(128)}, /*index=5*/s32[]{:T(128)}, s32[]{:T(128)}) while((s32[]{:T(128)}, bf16[5,6,6,4,2,256]{5,3,2,1,4,0:T(4,128)(2,1)S(1)}, s32[5,2]{0,1:T(2,128)S(1)}, ...), condition=%wide.region_3.4_spmd, body=%wide.region_0.3_spmd.sunk | while | flops 1499144 | bytes 2998465 | solution.py:39
  61.7 0.6 fusion.24
  66.2 0.9 add_reduce_fusion.2
  67.3 0.6 fusion.24
  71.9 0.9 add_reduce_fusion.2
  73.0 0.6 fusion.24
  77.6 0.9 add_reduce_fusion.2
  78.7 0.6 fusion.24
  83.3 0.9 add_reduce_fusion.2
  84.4 0.6 fusion.24
  89.0 0.9 add_reduce_fusion.2
  90.0 0.9 convert_reduce_fusion
  91.0 0.3 copy.26
  91.5 1.2 fusion.17
  92.8 32.7 %all-reduce.4.cloned.1.call-done = f32[180,512]{1,0:T(8,128)} async-done(((f32[180,512]{1,0:T(8,128)}), f32[180,512]{1,0:T(8,128)}) %all-reduce.4.cloned.1.call-update) | async-done | bytes 368656 | tf_op jit(solution)/shard_map/psum | solution.py:85
  125.4 1.3 convolution_multiply_fusion
  126.8 0.2 reshape.280
  127.0 0.3 fusion.16
  128.0 0.3 fusion.8
  128.3 0.3 convolution_add_fusion
  128.6 0.7 reshape.283
  129.3 0.6 dynamic-slice
  130.6 69.3 %all-reduce.6.cloned.1.call-done = f32[48,2,256]{2,1,0:T(2,128)} async-done(((f32[48,2,256]{2,1,0:T(2,128)}), f32[48,2,256]{2,1,0:T(2,128)}) %all-reduce.6.cloned.1.call-update) | async-done | bytes 98320
  199.9 1.3 constant_dynamic-slice_fusion.1
  (68 shorter events, 2.9 us)
Async XLA Ops:
  6.5 11.0 %copy-start.2 = (s32[5,2]{0,1:T(2,128)S(1)}, s32[5,2]{0,1:T(2,128)}, u32[]{:S(2)}) copy-start(s32[5,2]{0,1:T(2,128)} %param.7) | copy-start | bytes 124
  9.2 11.1 %copy-start.1 = (f32[5,6,6,512]{3,2,1,0:T(8,128)S(1)}, f32[5,6,6,512]{3,2,1,0:T(8,128)}, u32[]{:S(2)}) copy-start(f32[5,6,6,512]{3,2,1,0:T(8,128)} %param.6) | copy-start | bytes 1105924
  13.3 8.5 %all-to-all-start = ((bf16[4,2,6144]{2,1,0:T(2,128)(2,1)}), bf16[4,2,6144]{2,1,0:T(2,128)(2,1)S(1)}, u32[]{:S(2)}, u32[]{:S(2)}) async-start(bf16[4,2,6144]{2,1,0:T(2,128)(2,1)} %reshape.288), calls=%async_computation | async-start | bytes 196608 | tf_op jit(solution)/shard_map/all_to_all | solution.py:73
  17.6 107.9 %all-reduce.4.cloned.1.call-start = ((), (), s32[]{:S(2)}) async-start(), calls=%async_computation.1 | async-start | bytes 753664 | tf_op jit(solution)/shard_map/psum | solution.py:85
  28.4 33.2 %copy-start = (bf16[5,6,6,4,2,256]{5,3,2,1,4,0:T(4,128)(2,1)S(1)}, bf16[5,6,6,4,2,256]{5,3,2,1,4,0:T(4,128)(2,1)}, u32[]{:S(2)}) copy-start(bf16[5,6,6,4,2,256]{5,3,2,1,4,0:T(4,128)(2,1)} %custom-call) | copy-start | bytes 2211844
  92.7 107.2 %all-reduce.6.cloned.1.call-start = ((), (), s32[]{:S(2)}) async-start(), calls=%async_computation.2 | async-start | bytes 196608
  127.0 2.3 %copy-start.3 = (u32[32]{0:T(128)S(1)}, u32[32]{0:T(128)}, u32[]{:S(2)}) copy-start(u32[32]{0:T(128)} %constant.56) | copy-start | bytes 388
Sparse Core Ops, SparseCore 0:
  92.8 32.5 all-reduce.3
  129.4 70.4 all-reduce.5
where the time goes:
time: 209 us; the launch traced here: 208 us
  waiting for transfers between devices  103 us (49%)
  blocking collectives  33.1 us (16%)
  local copies, waits for them, and re-layouts  21.4 us (10%)
  loops' own time  19 us (9%)
  between operations  14.4 us (7%)
  other arithmetic  9.29 us (4%)
  starting transfers between devices  4.28 us (2%)
  matrix products  3.13 us (1%)
    unnamed x3, waiting for transfers between devices  69.4 us
    all_gather x1, blocking collectives, on_device(): gathered = lax.all_gather(local, 'sta', axis=0, tiled=True)  33.1 us
    psum x1, waiting for transfers between devices, on_device(): lag_sum = lax.psum(lag_terms, 'seg')  32.7 us
    another operation x1, loops' own time, slot_cross(): return lax.map(one_slot, starts_all)  19 us
    unnamed x15, local copies, waits for them, and re-layouts  13.6 us
    reduce_sum x5, other arithmetic, group_cross(): jnp.sum(left_real * right_real + left_imag * right_imag, axis=3)  4.73 us
    all_to_all x1, starting transfers between devices, on_device(): lax.all_to_all(spectra, 'seg', split_axis=3, concat_axis=1, tiled=True)  4.24 us
  transfers between devices with their start and end apart: 3, of which 3 were waited for; matrix products, arithmetic and copies ran while one was open for 2% of the time, Pallas kernels for 0%

commit v1 on v0

--- a/solution.py
+++ b/solution.py
@@ -82,7 +82,7 @@
         exact.reshape(2 * width, LAGS),
         precision=lax.Precision.HIGHEST,
     )
-    lag_sum = lax.psum(lag_terms, "seg")
+    lag_sum = jnp.sum(lax.all_gather(lag_terms, "seg"), axis=0)
     residual = (keep * jnp.tanh(scale * lag_sum - observe_flat)).astype(jnp.bfloat16)
     matrix = kernel.reshape(2 * width, LAGS)
     gamma = scale * lax.dot_general(

time: 209 us -> 196 us (0.938)
  waiting for transfers between devices: 103 us -> 90.1 us
    psum x1 -> x0, waiting for transfers between devices: 32.7 us -> none  [on_device(): lag_sum = lax.psum(lag_terms, 'seg')]
    all_gather x0 -> x1, waiting for transfers between devices: none -> 19.3 us  [on_device(): lag_sum = jnp.sum(lax.all_gather(lag_terms, 'seg'), axis=0)]
    another operation x0 -> x2, other arithmetic: none -> 2.51 us
    cos x1 -> x0, other arithmetic: 2.46 us -> none  [lag_kernel(): jnp.cos(angle)]
    unnamed x15 -> x13, local copies, waits for them, and re-layouts: 13.6 us -> 13.6 us
where the time goes in v1:
time: 196 us; the launch traced here: 195 us
  waiting for transfers between devices  90.1 us (46%)
  blocking collectives  32.9 us (17%)
  local copies, waits for them, and re-layouts  21.4 us (11%)
  loops' own time  19 us (10%)
  between operations  14.4 us (7%)
  other arithmetic  11.1 us (6%)
  starting transfers between devices  4.28 us (2%)
  matrix products  2.13 us (1%)
    unnamed x3, waiting for transfers between devices  69.1 us
    all_gather x1, blocking collectives, on_device(): gathered = lax.all_gather(local, 'sta', axis=0, tiled=True)  32.9 us
    all_gather x1, waiting for transfers between devices, on_device(): lag_sum = jnp.sum(lax.all_gather(lag_terms, 'seg'), axis=0)  19.3 us
    another operation x1, loops' own time, slot_cross(): return lax.map(one_slot, starts_all)  19 us
    unnamed x13, local copies, waits for them, and re-layouts  13.6 us
    reduce_sum x5, other arithmetic, group_cross(): jnp.sum(left_real * right_real + left_imag * right_imag, axis=3)  4.73 us
    all_to_all x1, starting transfers between devices, on_device(): lax.all_to_all(spectra, 'seg', split_axis=3, concat_axis=1, tiled=True)  4.24 us
  transfers between devices with their start and end apart: 3, of which 3 were waited for; matrix products, arithmetic and copies ran while one was open for 2% of the time, Pallas kernels for 0%

profile of v1, /device:TPU:0, one launch (start us, length us, event | category | flops | bytes accessed | tf_op | source)
XLA Modules:
  0.0 195.3 jit_solution(11775892495471226098)
XLA Ops:
  6.5 2.7 %copy.23 = bf16[6,4,2,1024]{0,1,2,3:T(4,128)(2,1)S(1)} copy(bf16[6,4,2,1024]{3,2,1,0:T(2,128)(2,1)} %param.5) | data formatting | bytes 196608 | tf_op args[0]
  9.2 4.1 %reshape.296 = bf16[4,2,6144]{2,1,0:T(2,128)(2,1)} reshape(bf16[1024,2,4,6]{3,2,1,0:T(4,128)(2,1)S(1)} %bitcast.67) | data formatting | bytes 196608
  13.3 4.2 %all-to-all-start = ((bf16[4,2,6144]{2,1,0:T(2,128)(2,1)}), bf16[4,2,6144]{2,1,0:T(2,128)(2,1)S(1)}, u32[]{:S(2)}, u32[]{:S(2)}) async-start(bf16[4,2,6144]{2,1,0:T(2,128)(2,1)} %reshape.296), calls=%async_computation | async-start | bytes 196608 | tf_op jit(solution)/shard_map/all_to_all | solution.py:73
  17.6 2.5 %cosine_convert_fusion = (bf16[1,256,512]{2,1,0:T(8,128)(2,1)S(1)}, bf16[1,256,512]{2,1,0:T(8,128)(2,1)S(1)}) fusion(s32[512]{0:T(512)S(1)} %iota_add_fusion, s32[256]{0:T(256)S(1)} %iota_add_fusion.1), kind=kLoop, calls=%fused_computation.26 | loop fusion | flops 2228224 | bytes 527360 | tf_op jit(solution)/shard_map/convert.6
  20.1 1.7 all-to-all-done
  21.9 4.7 %reshape.297 = bf16[1024,2,4,6]{3,2,1,0:T(4,128)(2,1)S(1)} reshape(bf16[4,2,6144]{2,1,0:T(2,128)(2,1)S(1)} %all-to-all-done) | data formatting | bytes 196608
  26.6 1.8 copy.24
  28.4 32.9 %all_gather.9 = bf16[48,16,2,256]{3,1,2,0:T(8,128)(2,1)S(1)} all-gather(bf16[6,16,2,256]{3,1,2,0:T(8,128)(2,1)S(1)} %all_to_all.16), channel_id=1, replica_groups=mesh['sta'=8,'seg'=4] {'sta'}, dimensions={0}, use_global_device_ids=true | all-gather | bytes 884736 | tf_op jit(solution)/shard_map/all_gather | solution.py:74
  61.4 28.5 %while.10 = (s32[]{:T(128)}, bf16[5,6,6,4,2,256]{5,3,2,1,4,0:T(4,128)(2,1)S(1)}, s32[5,2]{0,1:T(2,128)S(1)}, bf16[48,16,2,256]{3,1,0,2:T(8,128)(2,1)S(1)}, s32[]{:T(128)}, /*index=5*/s32[]{:T(128)}, s32[]{:T(128)}) while((s32[]{:T(128)}, bf16[5,6,6,4,2,256]{5,3,2,1,4,0:T(4,128)(2,1)S(1)}, s32[5,2]{0,1:T(2,128)S(1)}, ...), condition=%wide.region_3.4_spmd, body=%wide.region_0.3_spmd.sunk | while | flops 1499144 | bytes 2998473 | solution.py:39
  61.5 0.6 fusion.20
  66.1 0.9 add_reduce_fusion.2
  67.2 0.6 fusion.20
  71.8 0.9 add_reduce_fusion.2
  72.9 0.6 fusion.20
  77.5 0.9 add_reduce_fusion.2
  78.6 0.6 fusion.20
  83.1 0.9 add_reduce_fusion.2
  84.3 0.6 fusion.20
  88.8 0.9 add_reduce_fusion.2
  89.9 1.0 convert_reduce_fusion
  90.9 0.3 copy.26
  91.3 1.2 convolution_bitcast_fusion
  92.7 19.3 %all-gather.4.cloned.1.call-done = f32[4,180,512]{2,1,0:T(8,128)} async-done(((f32[1,180,512]{2,1,0:T(8,128)}), f32[4,180,512]{2,1,0:T(8,128)}) %all-gather.4.cloned.1.call-update) | async-done | bytes 1474576 | tf_op jit(solution)/shard_map/all_gather | solution.py:85
  112.0 1.6 reduce_sum.73
  113.9 0.3 convolution_multiply_fusion
  114.5 0.3 fusion.12
  115.5 0.3 fusion.5
  115.8 0.3 convolution_add_fusion
  116.1 0.7 reshape.288
  116.8 0.6 dynamic-slice
  118.1 69.1 %all-reduce.3.cloned.1.call-done = f32[48,2,256]{2,1,0:T(2,128)} async-done(((f32[48,2,256]{2,1,0:T(2,128)}), f32[48,2,256]{2,1,0:T(2,128)}) %all-reduce.3.cloned.1.call-update) | async-done | bytes 98320
  187.2 1.3 constant_dynamic-slice_fusion.1
  (69 shorter events, 3.3 us)
Async XLA Ops:
  6.5 11.1 %copy-start.1 = (s32[5,2]{0,1:T(2,128)S(1)}, s32[5,2]{0,1:T(2,128)}, u32[]{:S(2)}) copy-start(s32[5,2]{0,1:T(2,128)} %param.7) | copy-start | bytes 124
  13.3 8.5 %all-to-all-start = ((bf16[4,2,6144]{2,1,0:T(2,128)(2,1)}), bf16[4,2,6144]{2,1,0:T(2,128)(2,1)S(1)}, u32[]{:S(2)}, u32[]{:S(2)}) async-start(bf16[4,2,6144]{2,1,0:T(2,128)(2,1)} %reshape.296), calls=%async_computation | async-start | bytes 196608 | tf_op jit(solution)/shard_map/all_to_all | solution.py:73
  17.6 94.4 %all-gather.4.cloned.1.call-start = ((), (), s32[]{:S(2)}) async-start(), calls=%async_computation.1 | async-start | bytes 1884160 | tf_op jit(solution)/shard_map/all_gather | solution.py:85
  92.5 21.1 %copy-start = (f32[5,6,6,512]{3,2,1,0:T(8,128)S(1)}, f32[5,6,6,512]{3,2,1,0:T(8,128)}, u32[]{:S(2)}) copy-start(f32[5,6,6,512]{3,2,1,0:T(8,128)} %param.6) | copy-start | bytes 1105924
  92.6 94.6 %all-reduce.3.cloned.1.call-start = ((), (), s32[]{:S(2)}) async-start(), calls=%async_computation.2 | async-start | bytes 196608
  114.5 2.3 %copy-start.2 = (u32[32]{0:T(128)S(1)}, u32[32]{0:T(128)}, u32[]{:S(2)}) copy-start(u32[32]{0:T(128)} %constant.56) | copy-start | bytes 388
Sparse Core Ops, SparseCore 0:
  92.7 19.2 all-gather.3
  117.0 70.1 all-reduce.2
